TPU v7x, 32 devices: a whole 2x2x4 slice. The times are simulated.
32 devices in a mesh: half: 2 (over y), row: 4 (over z), col: 4 (over x, core).
Axes of the slice: x: 2, y: 2, z: 4, core: 2. Of those that a mesh axis runs over, the one named last changes fastest.
Arguments:
- front_init: float32 [10240, 10240], P(('half', 'row'), 'col'), may hold values from -2 to 8, as said below
- child_update: float32 [2, 8192, 8192], P('half', 'row', 'col'), may hold values from -2 to 8, as said below
- child_map: int32 [2, 8192], replicated, may hold values from 0 to 10239, as said below
Outputs:
- factor_front: float32 [10240, 10240], P(('half', 'row'), 'col')
Inputs may be any that keep to these rules, and one draw needn't show every extreme that they name: `child_map`: each child's entries are distinct. Each aligned block of 128 child indices maps onto one whole block of 128 front indices; write b(j) for the front block of child block j. For every r and q below 4, exactly 4 child blocks j with j % 4 == r have b(j) % 4 == q, and these share one value of b(j) % 8. Symmetric in natural order, and front_init minus the identity is positive semidefinite. `child_update`: each child's matrix is symmetric positive semidefinite.
All inputs are finite; a program needn't handle non-finite values.
Results may differ from a plain program's by a relative error of at most 0.0001.
Values sent between devices are 32-bit elements; how exact they have to be, the bound alone decides.
A program may use at most 256 MiB of HBM per device.

v0:
```python
import jax
import jax.numpy as jnp
from jax import lax
from jax.sharding import PartitionSpec as P

BLOCK_EDGE = 128
PANELS = 2
PANEL = 256


def column_order(which_map, source, grid_size, blocks_dev, slot_count):
    local_ids = jnp.arange(blocks_dev)
    targets = which_map[local_ids * grid_size + source] % grid_size
    return jnp.argsort(targets * blocks_dev + local_ids).reshape(grid_size, slot_count)


def row_slots(which_map, source, grid_size, group_count, blocks_dev, slot_count):
    local_ids = jnp.arange(blocks_dev)
    targets = which_map[local_ids * grid_size + source] % group_count
    onehot = targets[None, :] == jnp.arange(group_count)[:, None]
    ranking = jnp.cumsum(onehot.astype(jnp.int32), axis=1)
    matches = onehot[:, None, :] & (
        ranking[:, None, :] == jnp.arange(1, slot_count + 1)[None, :, None]
    )
    slot_index = jnp.sum(matches.astype(jnp.int32) * local_ids[None, None, :], axis=2)
    filled = jnp.any(matches, axis=2)
    return (slot_index, filled)


def on_device(front_init, child_update, child_map):
    grid_size = lax.axis_size("row")
    halves = lax.axis_size("half")
    group_count = halves * grid_size
    my_child = lax.axis_index("half")
    my_row = lax.axis_index("row")
    my_col = lax.axis_index("col")
    my_group = lax.axis_index(("half", "row"))
    child_rows = child_update.shape[1]
    blocks_dev = child_rows // BLOCK_EDGE
    slot_count = blocks_dev // grid_size
    front_rows, front_cols = front_init.shape
    row_blocks = front_rows // BLOCK_EDGE
    block_map = child_map.reshape(2, -1, BLOCK_EDGE)[:, :, 0] // BLOCK_EDGE
    inner_perm = child_map.reshape(2, -1, BLOCK_EDGE) % BLOCK_EDGE
    own_map = block_map[my_child]
    send_order = column_order(own_map, my_col, grid_size, blocks_dev, slot_count).reshape(-1)
    blocks = child_update[0].reshape(child_rows, blocks_dev, BLOCK_EDGE)
    outgoing = jnp.take(blocks, send_order, axis=1).reshape(child_rows, blocks_dev * BLOCK_EDGE)
    incoming = lax.all_to_all(outgoing, "col", split_axis=1, concat_axis=1, tiled=True)
    slot_index, filled = row_slots(own_map, my_row, grid_size, group_count, blocks_dev, slot_count)
    stacked = incoming.reshape(blocks_dev, BLOCK_EDGE, -1)
    packed = jnp.take(stacked, slot_index.reshape(-1), axis=0).reshape(
        group_count, slot_count, BLOCK_EDGE, -1
    )
    packed = jnp.where(filled[:, :, None, None], packed, 0.0).reshape(
        group_count * slot_count * BLOCK_EDGE, -1
    )
    arrived = lax.all_to_all(packed, ("half", "row"), split_axis=0, concat_axis=0, tiled=True)
    arrived = arrived.reshape(halves, grid_size * slot_count * BLOCK_EDGE, -1)
    front_local = front_init
    sources = jnp.arange(grid_size)
    for which_child in range(2):
        which_map = block_map[which_child]
        which_inner = inner_perm[which_child]
        orders = jax.vmap(
            lambda source: column_order(which_map, source, grid_size, blocks_dev, slot_count)
        )(sources)
        col_blocks = (orders[:, my_col, :] * grid_size + sources[:, None]).reshape(-1)
        col_index = (
            (which_map[col_blocks] // grid_size * BLOCK_EDGE)[:, None] + which_inner[col_blocks]
        ).reshape(-1)
        slot_all, fill_all = jax.vmap(
            lambda source: row_slots(
                which_map, source, grid_size, group_count, blocks_dev, slot_count
            )
        )(sources)
        mine_slot = slot_all[:, my_group, :]
        mine_fill = fill_all[:, my_group, :]
        child_blocks = mine_slot * grid_size + sources[:, None]
        target_blocks = which_map[child_blocks]
        row_index = (target_blocks // group_count * BLOCK_EDGE)[:, :, None] + which_inner[
            child_blocks
        ]
        row_index = jnp.where(mine_fill[:, :, None], row_index, front_rows).reshape(-1)
        spread = (
            jnp.zeros((arrived.shape[1], front_cols), jnp.float32)
            .at[:, col_index]
            .set(arrived[which_child])
        )
        front_local = front_local.at[row_index].add(spread, mode="drop")
    row_ids = jnp.arange(front_rows)
    natural_rows = (
        row_ids // BLOCK_EDGE * group_count + my_group
    ) * BLOCK_EDGE + row_ids % BLOCK_EDGE
    col_ids = jnp.arange(front_cols)
    natural_cols = (col_ids // BLOCK_EDGE * grid_size + my_col) * BLOCK_EDGE + col_ids % BLOCK_EDGE
    identity = jnp.eye(PANEL, dtype=jnp.float32)
    for panel_index in range(PANELS):
        panel_start = panel_index * PANEL
        panel_end = panel_start + PANEL
        panel_slab = lax.all_gather(front_local[:, :BLOCK_EDGE], "col", axis=1, tiled=True)[
            :, panel_start:panel_end
        ]
        pieces = []
        for block_part in range(PANEL // BLOCK_EDGE):
            owner_group = (panel_start // BLOCK_EDGE + block_part) % group_count
            pieces.append(jnp.where(my_group == owner_group, panel_slab[:BLOCK_EDGE], 0.0))
        diagonal = lax.psum(jnp.concatenate(pieces, axis=0), ("half", "row"))
        factor = jnp.linalg.cholesky(diagonal)
        inverse = lax.linalg.triangular_solve(factor, identity, left_side=True, lower=True)
        panel_rows = jnp.dot(panel_slab, inverse.T, precision=lax.Precision.HIGHEST)
        panel_rows = jnp.where((natural_rows >= panel_start)[:, None], panel_rows, 0.0)
        everything = lax.all_gather(panel_rows, ("half", "row"), axis=0, tiled=True)
        everything = everything.reshape(halves, grid_size, row_blocks, BLOCK_EDGE, PANEL)
        selected = lax.dynamic_index_in_dim(everything, my_col, axis=1, keepdims=False)
        column_panel = selected.transpose(1, 0, 2, 3).reshape(front_cols, PANEL)
        update = jnp.dot(panel_rows, column_panel.T, precision=lax.Precision.HIGHEST)
        trailing = (natural_rows >= panel_end)[:, None] & (natural_cols >= panel_end)[None, :]
        front_local = jnp.where(trailing, front_local - update, front_local)
        in_panel = (natural_cols >= panel_start) & (natural_cols < panel_end)
        panel_values = jnp.take(
            panel_rows, jnp.clip(natural_cols - panel_start, 0, PANEL - 1), axis=1
        )
        front_local = jnp.where(in_panel[None, :], panel_values, front_local)
        upper_zero = ((natural_rows >= panel_start) & (natural_rows < panel_end))[:, None] & (
            natural_cols >= panel_end
        )[None, :]
        front_local = jnp.where(upper_zero, 0.0, front_local)
    return front_local


def solution(mesh):
    placed = (P(("half", "row"), "col"), P("half", "row", "col"), P())
    return jax.shard_map(
        on_device, mesh=mesh, in_specs=placed, out_specs=P(("half", "row"), "col"), check_vma=False
    )
```

profile of v0, /device:TPU:0, one launch (start us, length us, event | category | flops | bytes accessed | tf_op | source)
XLA Modules:
  0.0 2033.6 jit_solution(14741416370974196072)
XLA Ops:
  20.2 17.6 copy.111
  37.8 17.6 copy.112
  55.4 13.8 gather_fusion.7
  69.2 17.6 copy.113
  106.3 182.7 %all-to-all-done = f32[2048,4,512]{0,2,1:T(8,128)} async-done(((f32[2048,4,512]{0,2,1:T(8,128)}), f32[2048,4,512]{0,2,1:T(8,128)}, u32[]{:S(2)}, u32[]{:S(2)}) %all-to-all-start) | async-done | bytes 16777248 | tf_op jit(solution)/shard_map/all_to_all | solution.py:49
  289.0 14.1 copy.151
  303.1 18.0 copy.142
  321.2 18.8 gather_fusion.8
  340.0 23.1 %fusion = f32[8,512,2048]{2,1,0:T(8,128)} fusion(pred[8,512]{1,0:T(8,128)(4,1)S(1)} %broadcast_bitcast_fusion, pred[8,512]{1,0:T(8,128)(4,1)S(1)} %broadcast_bitcast_fusion.1, f32[8,512,2048]{2,1,0:T(8,128)} %bitcast.166), kind=kLoop, calls=%fused_computation.25 | loop fusion | flops 16777216 | bytes 67117056 | tf_op jit(solution)/shard_map/jit(_where)/select_n | solution.py:55
  384.7 709.6 %all-to-all-done.1 = f32[8,512,2048]{2,1,0:T(8,128)} async-done(((f32[8,512,2048]{2,1,0:T(8,128)}), f32[8,512,2048]{2,1,0:T(8,128)}, u32[]{:S(2)}, u32[]{:S(2)}) %all-to-all-start.1) | async-done | bytes 33554464 | tf_op jit(solution)/shard_map/all_to_all | solution.py:58
  1094.3 21.1 %fusion.91 = (f32[4,512,2048]{2,1,0:T(8,128)}, f32[4,512,2048]{2,1,0:T(8,128)}) fusion(f32[8,512,2048]{2,1,0:T(8,128)} %all-to-all-done.1), kind=kLoop, calls=%fused_computation.286 | loop fusion | bytes 67108864 | tf_op jit(solution)/shard_map/slice | solution.py:88
  1115.4 17.6 copy.143
  1133.0 21.8 %scatter_custom_fusion = f32[2048,2560]{0,1:T(8,128)} fusion(s32[2048]{0:T(1024)S(1)} %bitcast.190, f32[2048,2048]{0,1:T(8,128)} %copy.143, f32[]{:T(128)} %constant.323.clone.1), kind=kCustom, calls=%fused_computation.30 | custom fusion | bytes 37748740 | tf_op jit(solution)/shard_map/scatter | solution.py:88
  1154.9 20.0 copy.117
  1174.8 17.6 copy.146
  1192.4 21.9 %scatter_custom_fusion.2 = f32[2048,2560]{0,1:T(8,128)} fusion(s32[2048]{0:T(1024)S(1)} %bitcast.189, f32[2048,2048]{0,1:T(8,128)} %copy.146, f32[]{:T(128)} %constant.323.clone.1), kind=kCustom, calls=%fused_computation.28 | custom fusion | bytes 37748740 | tf_op jit(solution)/shard_map/scatter | solution.py:88
  1214.3 19.9 copy.125
  1234.3 42.9 %scatter_fusion = f32[1280,2560]{1,0:T(8,128)} fusion(f32[1280,2560]{1,0:T(8,128)} %copy.186, s32[2048]{0:T(1024)S(1)} %bitcast.180, f32[2048,2560]{1,0:T(8,128)} %copy.117), kind=kCustom, calls=%fused_computation.17 | custom fusion | flops 5242880 | bytes 62922752 | tf_op jit(solution)/shard_map/scatter-add | solution.py:90
  1277.2 42.5 %scatter_fusion.1 = f32[1280,2560]{1,0:T(8,128)} fusion(f32[1280,2560]{1,0:T(8,128)} %scatter_fusion, s32[2048]{0:T(1024)S(1)} %bitcast.181, f32[2048,2560]{1,0:T(8,128)} %copy.125), kind=kCustom, calls=%fused_computation.19 | custom fusion | flops 5242880 | bytes 62922752 | tf_op jit(solution)/shard_map/scatter-add | solution.py:90
  1319.7 14.0 copy.126
  1335.7 22.0 %all-gather.5.cloned.1.call-done = f32[1280,512]{0,1:T(8,128)} async-done(((f32[1280,128]{0,1:T(8,128)}), f32[1280,512]{0,1:T(8,128)}) %all-gather.5.cloned.1.call-update) | async-done | bytes 2621456 | tf_op jit(solution)/shard_map/all_gather | solution.py:101
  1359.7 72.0 %all-reduce.4.cloned.1.call-done = f32[256,256]{0,1:T(8,128)} async-done(((f32[256,256]{0,1:T(8,128)}), f32[256,256]{0,1:T(8,128)}) %all-reduce.4.cloned.1.call-update) | async-done | bytes 262160 | tf_op jit(solution)/shard_map/psum | solution.py:108
  1455.8 11.7 cholesky.147
  1474.5 19.7 custom-call.14
  1511.3 138.7 %all-gather.7.cloned.1.call-done = f32[10240,256]{1,0:T(8,128)} async-done(((f32[1280,256]{1,0:T(8,128)}), f32[10240,256]{1,0:T(8,128)}) %all-gather.7.cloned.1.call-update) | async-done | bytes 10485776 | tf_op jit(solution)/shard_map/all_gather | solution.py:113
  1652.3 19.9 fusion.6
  1674.2 23.8 %all-gather.9.cloned.1.call-done = f32[1280,512]{0,1:T(8,128)} async-done(((f32[1280,128]{0,1:T(8,128)}), f32[1280,512]{0,1:T(8,128)}) %all-gather.9.cloned.1.call-update) | async-done | bytes 2621456 | tf_op jit(solution)/shard_map/all_gather | solution.py:101
  1700.2 72.0 %all-reduce.6.cloned.1.call-done = f32[256,256]{0,1:T(8,128)} async-done(((f32[256,256]{0,1:T(8,128)}), f32[256,256]{0,1:T(8,128)}) %all-reduce.6.cloned.1.call-update) | async-done | bytes 262160 | tf_op jit(solution)/shard_map/psum | solution.py:108
  1814.9 19.7 custom-call.16
  1851.9 138.5 %all-gather.11.cloned.1.call-done = f32[10240,256]{1,0:T(8,128)} async-done(((f32[1280,256]{1,0:T(8,128)}), f32[10240,256]{1,0:T(8,128)}) %all-gather.11.cloned.1.call-update) | async-done | bytes 10485776 | tf_op jit(solution)/shard_map/all_gather | solution.py:113
  1992.7 19.9 fusion.8
  2012.6 13.9 copy.137
  (202 shorter events, 180.4 us)
Async XLA Ops:
  6.5 10.8 copy-start.2
  98.4 190.7 %all-to-all-start = ((f32[2048,4,512]{0,2,1:T(8,128)}), f32[2048,4,512]{0,2,1:T(8,128)}, u32[]{:S(2)}, u32[]{:S(2)}) async-start(f32[2048,4,512]{0,2,1:T(8,128)} %bitcast_select_fusion.1), calls=%async_computation | async-start | bytes 33554432 | tf_op jit(solution)/shard_map/all_to_all | solution.py:49
  363.1 731.2 %all-to-all-start.1 = ((f32[8,512,2048]{2,1,0:T(8,128)}), f32[8,512,2048]{2,1,0:T(8,128)}, u32[]{:S(2)}, u32[]{:S(2)}) async-start(f32[8,512,2048]{2,1,0:T(8,128)} %fusion), calls=%async_computation.1 | async-start | bytes 67108864 | tf_op jit(solution)/shard_map/all_to_all | solution.py:58
  370.1 987.6 %all-gather.5.cloned.1.call-start = ((), (), s32[]{:S(2)}) async-start(), calls=%async_computation.2 | async-start | bytes 3276800 | tf_op jit(solution)/shard_map/all_gather | solution.py:101
  1234.3 42.9 %copy-start.3 = (s32[2048,1]{0,1:T(1,128)S(1)}, s32[2048,1]{0,1:T(1,128)}, u32[]{:S(2)}) copy-start(s32[2048,1]{0,1:T(1,128)} %compare_select_fusion.1) | copy-start | bytes 24580
  1335.6 96.0 %all-reduce.4.cloned.1.call-start = ((), (), s32[]{:S(2)}) async-start(), calls=%async_computation.3 | async-start | bytes 524288 | tf_op jit(solution)/shard_map/psum | solution.py:108
  1359.4 290.6 %all-gather.7.cloned.1.call-start = ((), (), s32[]{:S(2)}) async-start(), calls=%async_computation.4 | async-start | bytes 11796480 | tf_op jit(solution)/shard_map/all_gather | solution.py:113
  1499.7 198.3 %all-gather.9.cloned.1.call-start = ((), (), s32[]{:S(2)}) async-start(), calls=%async_computation.5 | async-start | bytes 3276800 | tf_op jit(solution)/shard_map/all_gather | solution.py:101
  1501.6 150.7 %copy-start.1 = (f32[1280,256]{1,0:T(8,128)S(1)}, f32[1280,256]{1,0:T(8,128)}, u32[]{:S(2)}) copy-start(f32[1280,256]{1,0:T(8,128)} %convolution_select_fusion.1) | copy-start | bytes 3932164
  1674.2 98.0 %all-reduce.6.cloned.1.call-start = ((), (), s32[]{:S(2)}) async-start(), calls=%async_computation.6 | async-start | bytes 524288 | tf_op jit(solution)/shard_map/psum | solution.py:108
  1699.8 290.7 %all-gather.11.cloned.1.call-start = ((), (), s32[]{:S(2)}) async-start(), calls=%async_computation.7 | async-start | bytes 11796480 | tf_op jit(solution)/shard_map/all_gather | solution.py:113
  1842.0 150.7 %copy-start = (f32[1280,256]{1,0:T(8,128)S(1)}, f32[1280,256]{1,0:T(8,128)}, u32[]{:S(2)}) copy-start(f32[1280,256]{1,0:T(8,128)} %convolution_select_fusion) | copy-start | bytes 3932164
Sparse Core Ops, SparseCore 0:
  1335.7 21.9 all-gather.4
  1361.1 70.5 all-reduce.3
  1499.9 150.1 all-gather.6
  1674.3 23.7 all-gather.8
  1701.6 70.5 all-reduce.5
  1840.3 150.1 all-gather.10
where the time goes:
time: 2040 us; the launch traced here: 2030 us
  waiting for transfers between devices  1360 us (67%)
  local copies, waits for them, and re-layouts  348 us (17%)
  other arithmetic  242 us (12%)
  matrix products  51.8 us (3%)
    all_to_all x1, waiting for transfers between devices, on_device(): lax.all_to_all(packed, ('half', 'row'), split_axis=0, concat_axis=0, tile...  710 us
    all_gather x2, waiting for transfers between devices, on_device(): everything = lax.all_gather(panel_rows, ('half', 'row'), axis=0, tiled=True)  277 us
    all_to_all x1, waiting for transfers between devices, on_device(): lax.all_to_all(outgoing, 'col', split_axis=1, concat_axis=1, tiled=True)  183 us
    psum x2, waiting for transfers between devices, on_device(): diagonal = lax.psum(jnp.concatenate(pieces, axis=0), ('half', 'row'))  144 us
    scatter-add x2, other arithmetic, on_device(): front_local = front_local.at[row_index].add(spread, mode='drop')  85.4 us
    scatter x4, local copies, waits for them, and re-layouts, on_device(): spread = jnp.zeros((arrived.shape[1], front_cols), jnp.float32).at[:, col...  83.6 us
    another operation x14, other arithmetic, on_device(): factor = jnp.linalg.cholesky(diagonal)  69.3 us
    slice x3, local copies, waits for them, and re-layouts, on_device(): arrived[which_child]  56.4 us
  transfers between devices with their start and end apart: 8, of which 8 were waited for; matrix products, arithmetic and copies ran while one was open for 2% of the time, Pallas kernels for 0%

commit v1 on v0

--- a/solution.py
+++ b/solution.py
@@ -105,7 +105,9 @@
         for block_part in range(PANEL // BLOCK_EDGE):
             owner_group = (panel_start // BLOCK_EDGE + block_part) % group_count
             pieces.append(jnp.where(my_group == owner_group, panel_slab[:BLOCK_EDGE], 0.0))
-        diagonal = lax.psum(jnp.concatenate(pieces, axis=0), ("half", "row"))
+        block = jnp.concatenate(pieces, axis=0)
+        parts = lax.all_gather(block, ("half", "row"), axis=0, tiled=False)
+        diagonal = parts.sum(axis=0)
         factor = jnp.linalg.cholesky(diagonal)
         inverse = lax.linalg.triangular_solve(factor, identity, left_side=True, lower=True)
         panel_rows = jnp.dot(panel_slab, inverse.T, precision=lax.Precision.HIGHEST)

time: 2040 us -> 1970 us (0.966)
  waiting for transfers between devices: 1360 us -> 1280 us
    psum x2 -> x0, waiting for transfers between devices: 144 us -> none  [on_device(): diagonal = lax.psum(jnp.concatenate(pieces, axis=0), ('half', 'row'))]
    all_gather x0 -> x2, waiting for transfers between devices: none -> 98.6 us  [on_device(): parts = lax.all_gather(block, ('half', 'row'), axis=0, tiled=False)]
    all_gather x2, waiting for transfers between devices: 277 us -> 247 us  [on_device(): everything = lax.all_gather(panel_rows, ('half', 'row'), axis=0, tiled=True)]
    gather x2 -> x4, local copies, waits for them, and re-layouts: 19.6 us -> 47.9 us  [on_device(): jnp.take(panel_rows, jnp.clip(natural_cols - panel_start, 0, PANEL - 1),...]
  transfers between devices with their start and end apart: 8 -> 8, of which waited for: 8 -> 8; matrix products, arithmetic and copies ran while one was open for 2% -> 3% of each run, Pallas kernels for 0% -> 0%
where the time goes in v1:
time: 1970 us; the launch traced here: 1960 us
  waiting for transfers between devices  1280 us (65%)
  local copies, waits for them, and re-layouts  346 us (18%)
  other arithmetic  244 us (12%)
  matrix products  51.3 us (3%)
    all_to_all x1, waiting for transfers between devices, on_device(): lax.all_to_all(packed, ('half', 'row'), split_axis=0, concat_axis=0, tile...  710 us
    all_gather x2, waiting for transfers between devices, on_device(): everything = lax.all_gather(panel_rows, ('half', 'row'), axis=0, tiled=True)  247 us
    all_to_all x1, waiting for transfers between devices, on_device(): lax.all_to_all(outgoing, 'col', split_axis=1, concat_axis=1, tiled=True)  183 us
    all_gather x2, waiting for transfers between devices, on_device(): parts = lax.all_gather(block, ('half', 'row'), axis=0, tiled=False)  98.6 us
    scatter-add x2, other arithmetic, on_device(): front_local = front_local.at[row_index].add(spread, mode='drop')  85.4 us
    scatter x4, local copies, waits for them, and re-layouts, on_device(): spread = jnp.zeros((arrived.shape[1], front_cols), jnp.float32).at[:, col...  83.6 us
    another operation x14, other arithmetic, on_device(): factor = jnp.linalg.cholesky(diagonal)  69.3 us
    slice x3, local copies, waits for them, and re-layouts, on_device(): arrived[which_child]  56.4 us
  transfers between devices with their start and end apart: 8, of which 8 were waited for; matrix products, arithmetic and copies ran while one was open for 3% of the time, Pallas kernels for 0%

profile of v1, /device:TPU:0, one launch (start us, length us, event | category | flops | bytes accessed | tf_op | source)
XLA Modules:
  0.0 1958.5 jit_solution(4318899226410002754)
XLA Ops:
  20.2 17.6 copy.125
  37.8 17.6 copy.126
  55.4 13.8 gather_fusion.7
  69.2 17.6 copy.127
  106.3 182.7 %all-to-all-done = f32[2048,4,512]{0,2,1:T(8,128)} async-done(((f32[2048,4,512]{0,2,1:T(8,128)}), f32[2048,4,512]{0,2,1:T(8,128)}, u32[]{:S(2)}, u32[]{:S(2)}) %all-to-all-start) | async-done | bytes 16777248 | tf_op jit(solution)/shard_map/all_to_all | solution.py:49
  289.0 14.1 copy.159
  303.1 18.0 copy.150
  321.2 18.8 gather_fusion.8
  340.0 23.1 %fusion = f32[8,512,2048]{2,1,0:T(8,128)} fusion(pred[8,512]{1,0:T(8,128)(4,1)S(1)} %broadcast_bitcast_fusion, pred[8,512]{1,0:T(8,128)(4,1)S(1)} %broadcast_bitcast_fusion.1, f32[8,512,2048]{2,1,0:T(8,128)} %bitcast.168), kind=kLoop, calls=%fused_computation.25 | loop fusion | flops 16777216 | bytes 67117056 | tf_op jit(solution)/shard_map/jit(_where)/select_n | solution.py:55
  384.7 709.6 %all-to-all-done.1 = f32[8,512,2048]{2,1,0:T(8,128)} async-done(((f32[8,512,2048]{2,1,0:T(8,128)}), f32[8,512,2048]{2,1,0:T(8,128)}, u32[]{:S(2)}, u32[]{:S(2)}) %all-to-all-start.1) | async-done | bytes 33554464 | tf_op jit(solution)/shard_map/all_to_all | solution.py:58
  1094.3 21.1 %fusion.91 = (f32[4,512,2048]{2,1,0:T(8,128)}, f32[4,512,2048]{2,1,0:T(8,128)}) fusion(f32[8,512,2048]{2,1,0:T(8,128)} %all-to-all-done.1), kind=kLoop, calls=%fused_computation.286 | loop fusion | bytes 67108864 | tf_op jit(solution)/shard_map/slice | solution.py:88
  1115.4 17.6 copy.151
  1133.0 21.8 %scatter_custom_fusion = f32[2048,2560]{0,1:T(8,128)} fusion(s32[2048]{0:T(1024)S(1)} %bitcast.194, f32[2048,2048]{0,1:T(8,128)} %copy.151, f32[]{:T(128)} %constant.323.clone.1), kind=kCustom, calls=%fused_computation.30 | custom fusion | bytes 37748740 | tf_op jit(solution)/shard_map/scatter | solution.py:88
  1154.9 20.0 %copy.131 = f32[2048,2560]{1,0:T(8,128)} copy(f32[2048,2560]{0,1:T(8,128)} %scatter_custom_fusion) | data formatting | bytes 41943040 | tf_op jit(solution)/shard_map/scatter | solution.py:88
  1174.8 17.6 copy.154
  1192.4 21.9 %scatter_custom_fusion.2 = f32[2048,2560]{0,1:T(8,128)} fusion(s32[2048]{0:T(1024)S(1)} %bitcast.193, f32[2048,2048]{0,1:T(8,128)} %copy.154, f32[]{:T(128)} %constant.323.clone.1), kind=kCustom, calls=%fused_computation.28 | custom fusion | bytes 37748740 | tf_op jit(solution)/shard_map/scatter | solution.py:88
  1214.3 19.9 %copy.139 = f32[2048,2560]{1,0:T(8,128)} copy(f32[2048,2560]{0,1:T(8,128)} %scatter_custom_fusion.2) | data formatting | bytes 41943040 | tf_op jit(solution)/shard_map/scatter | solution.py:88
  1234.3 42.9 %scatter_fusion = f32[1280,2560]{1,0:T(8,128)} fusion(f32[1280,2560]{1,0:T(8,128)} %copy.194, s32[2048]{0:T(1024)S(1)} %bitcast.184, f32[2048,2560]{1,0:T(8,128)} %copy.131), kind=kCustom, calls=%fused_computation.17 | custom fusion | flops 5242880 | bytes 62922752 | tf_op jit(solution)/shard_map/scatter-add | solution.py:90
  1277.2 42.5 %scatter_fusion.1 = f32[1280,2560]{1,0:T(8,128)} fusion(f32[1280,2560]{1,0:T(8,128)} %scatter_fusion, s32[2048]{0:T(1024)S(1)} %bitcast.185, f32[2048,2560]{1,0:T(8,128)} %copy.139), kind=kCustom, calls=%fused_computation.19 | custom fusion | flops 5242880 | bytes 62922752 | tf_op jit(solution)/shard_map/scatter-add | solution.py:90
  1321.7 22.4 %all-gather.9.cloned.1.call-done = f32[1280,512]{1,0:T(8,128)} async-done(((f32[1280,128]{1,0:T(8,128)}), f32[1280,512]{1,0:T(8,128)}) %all-gather.9.cloned.1.call-update) | async-done | bytes 2621456 | tf_op jit(solution)/shard_map/all_gather | solution.py:101
  1346.0 49.5 %all-gather.17.cloned.1.call-done = f32[2048,256]{1,0:T(8,128)} async-done(((f32[256,256]{1,0:T(8,128)}), f32[2048,256]{1,0:T(8,128)}) %all-gather.17.cloned.1.call-update) | async-done | bytes 2097168 | tf_op jit(solution)/shard_map/all_gather | solution.py:109
  1419.5 11.7 cholesky.147
  1438.2 19.7 %custom-call.14 = f32[2,128,128]{1,2,0:T(8,128)S(1)} custom-call(f32[2,128,128]{2,1,0:T(8,128)S(1)} %get-tuple-element.28), custom_call_target="InvertDiagBlocksLowerTriangular" | custom-call | tf_op jit(solution)/shard_map/triangular_solve/custom-call.0 | solution.py:112
  1474.2 14.1 copy.142
  1488.3 123.7 %all-gather.11.cloned.1.call-done = f32[10240,256]{1,0:T(8,128)} async-done(((f32[1280,256]{1,0:T(8,128)}), f32[10240,256]{1,0:T(8,128)}) %all-gather.11.cloned.1.call-update) | async-done | bytes 10485776 | tf_op jit(solution)/shard_map/all_gather | solution.py:115
  1614.1 20.7 %fusion.6 = f32[1280,2560]{1,0:T(8,128)} fusion(f32[1280,2560]{1,0:T(8,128)} %scatter_fusion.1, f32[1280,256]{1,0:T(8,128)S(1)} %copy-done.1, f32[2560,256]{1,0:T(8,128)S(1)} %bitcast.176, f32[2560,1280]{0,1:T(8,128)} %copy.142, pred[2560]{0:T(1024)(128)(4,1)S(1)} %get-tuple-element.97, pred[2560]{0:T(1024)(128)(4,1)S(1)} %get-tuple-element.98, ...), kind=kOutput, calls=%fused_computation.34 | convolution fusion | flops 10089267200 | bytes 43264000 | tf_op jit(solution)/shard_map/dot_general | solution.py:119
  1636.8 24.2 %all-gather.13.cloned.1.call-done = f32[1280,512]{1,0:T(8,128)} async-done(((f32[1280,128]{1,0:T(8,128)}), f32[1280,512]{1,0:T(8,128)}) %all-gather.13.cloned.1.call-update) | async-done | bytes 2621456 | tf_op jit(solution)/shard_map/all_gather | solution.py:101
  1663.1 49.2 %all-gather.19.cloned.1.call-done = f32[2048,256]{1,0:T(8,128)} async-done(((f32[256,256]{1,0:T(8,128)}), f32[2048,256]{1,0:T(8,128)}) %all-gather.19.cloned.1.call-update) | async-done | bytes 2097168 | tf_op jit(solution)/shard_map/all_gather | solution.py:109
  1754.8 19.7 %custom-call.16 = f32[2,128,128]{1,2,0:T(8,128)S(1)} custom-call(f32[2,128,128]{2,1,0:T(8,128)S(1)} %get-tuple-element.29), custom_call_target="InvertDiagBlocksLowerTriangular" | custom-call | tf_op jit(solution)/shard_map/triangular_solve/custom-call.0 | solution.py:112
  1790.8 14.1 copy.146
  1804.9 123.7 %all-gather.15.cloned.1.call-done = f32[10240,256]{1,0:T(8,128)} async-done(((f32[1280,256]{1,0:T(8,128)}), f32[10240,256]{1,0:T(8,128)}) %all-gather.15.cloned.1.call-update) | async-done | bytes 10485776 | tf_op jit(solution)/shard_map/all_gather | solution.py:115
  1930.8 20.7 %fusion.8 = f32[1280,2560]{1,0:T(8,128)} fusion(f32[1280,2560]{1,0:T(8,128)} %fusion.6, f32[1280,256]{1,0:T(8,128)S(1)} %copy-done, f32[2560,256]{1,0:T(8,128)S(1)} %bitcast.175, f32[2560,1280]{0,1:T(8,128)} %copy.146, pred[2560]{0:T(1024)(128)(4,1)S(1)} %get-tuple-element.95, pred[2560]{0:T(1024)(128)(4,1)S(1)} %get-tuple-element.96, ...), kind=kOutput, calls=%fused_computation.36 | convolution fusion | flops 10089267200 | bytes 43264000 | tf_op jit(solution)/shard_map/dot_general | solution.py:119
  (204 shorter events, 178.0 us)
Async XLA Ops:
  6.5 10.8 copy-start.2
  98.4 190.7 %all-to-all-start = ((f32[2048,4,512]{0,2,1:T(8,128)}), f32[2048,4,512]{0,2,1:T(8,128)}, u32[]{:S(2)}, u32[]{:S(2)}) async-start(f32[2048,4,512]{0,2,1:T(8,128)} %bitcast_select_fusion.1), calls=%async_computation | async-start | bytes 33554432 | tf_op jit(solution)/shard_map/all_to_all | solution.py:49
  363.1 731.2 %all-to-all-start.1 = ((f32[8,512,2048]{2,1,0:T(8,128)}), f32[8,512,2048]{2,1,0:T(8,128)}, u32[]{:S(2)}, u32[]{:S(2)}) async-start(f32[8,512,2048]{2,1,0:T(8,128)} %fusion), calls=%async_computation.1 | async-start | bytes 67108864 | tf_op jit(solution)/shard_map/all_to_all | solution.py:58
  370.1 973.9 %all-gather.9.cloned.1.call-start = ((), (), s32[]{:S(2)}) async-start(), calls=%async_computation.2 | async-start | bytes 3276800 | tf_op jit(solution)/shard_map/all_gather | solution.py:101
  1234.3 42.9 %copy-start.3 = (s32[2048,1]{0,1:T(1,128)S(1)}, s32[2048,1]{0,1:T(1,128)}, u32[]{:S(2)}) copy-start(s32[2048,1]{0,1:T(1,128)} %compare_select_fusion.1) | copy-start | bytes 24580
  1321.7 73.9 %all-gather.17.cloned.1.call-start = ((), (), s32[]{:S(2)}) async-start(), calls=%async_computation.6 | async-start | bytes 2359296 | tf_op jit(solution)/shard_map/all_gather | solution.py:109
  1345.8 266.2 %all-gather.11.cloned.1.call-start = ((), (), s32[]{:S(2)}) async-start(), calls=%async_computation.3 | async-start | bytes 11796480 | tf_op jit(solution)/shard_map/all_gather | solution.py:115
  1462.4 198.6 %all-gather.13.cloned.1.call-start = ((), (), s32[]{:S(2)}) async-start(), calls=%async_computation.4 | async-start | bytes 3276800 | tf_op jit(solution)/shard_map/all_gather | solution.py:101
  1474.2 140.0 %copy-start.1 = (f32[1280,256]{1,0:T(8,128)S(1)}, f32[1280,256]{1,0:T(8,128)}, u32[]{:S(2)}) copy-start(f32[1280,256]{1,0:T(8,128)} %convolution_select_fusion.1) | copy-start | bytes 3932164
  1636.8 75.5 %all-gather.19.cloned.1.call-start = ((), (), s32[]{:S(2)}) async-start(), calls=%async_computation.7 | async-start | bytes 2359296 | tf_op jit(solution)/shard_map/all_gather | solution.py:109
  1662.7 265.9 %all-gather.15.cloned.1.call-start = ((), (), s32[]{:S(2)}) async-start(), calls=%async_computation.5 | async-start | bytes 11796480 | tf_op jit(solution)/shard_map/all_gather | solution.py:115
  1790.8 140.0 %copy-start = (f32[1280,256]{1,0:T(8,128)S(1)}, f32[1280,256]{1,0:T(8,128)}, u32[]{:S(2)}) copy-start(f32[1280,256]{1,0:T(8,128)} %convolution_select_fusion) | copy-start | bytes 3932164
Sparse Core Ops, SparseCore 0:
  1321.8 22.2 all-gather.8
  1346.2 49.2 all-gather.16
  1462.5 149.3 all-gather.10
  1636.9 24.0 all-gather.12
  1663.0 49.2 all-gather.18
  1779.2 149.3 all-gather.14
